TPU v7x, 32 devices: a whole 2x2x4 slice. The times are simulated.
32 devices in a mesh: along: 2 (over core), across: 4 (over y, x), chan: 4 (over z).
Axes of the slice: x: 2, y: 2, z: 4, core: 2. Of those that a mesh axis runs over, the one named last changes fastest.
Arguments:
- jacobian: float32 [8, 32, 512, 384], P('along', 'across', 'chan'), may hold values from -0.3125 to 0.3125
- departures: float32 [8, 32, 512], P('along', 'across', 'chan'), may hold values from -6 to 6
- inv_variance: float32 [512], P('chan'), may hold values from 0.3 to 3
- channel_use: int32 [512], P('chan'), may hold values 0 or 1
- clear_flags: int32 [8, 32], P('along', 'across'), may hold values 0 or 1
- coefficients: float32 [25, 384], replicated, may hold values from -1.25 to 1.25
Outputs:
- control: float32 [8, 32, 384], P('along', 'across')
- increment: float32 [8, 32, 384], P('along', 'across')
- residual: float32 [8, 32, 384], P('along', 'across')
All inputs are finite; a program needn't handle non-finite values. No bound on the sum of `channel_use` or of `clear_flags` on one device may be relied on, other than what follows from the above.
Results may differ from a plain program's by a relative error of at most 0.0003.
Values sent between devices are 32-bit elements; how exact they have to be, the bound alone decides.
A program may use at most 64 MiB of HBM per device.

v0:
```python
import jax
import jax.numpy as jnp
from jax import lax
from jax.sharding import PartitionSpec as P

ITERS = 10


def extended(cells, sides, width):
    for axis, dim in sides:
        count = lax.axis_size(axis)
        ends = count - 1
        head = lax.slice_in_dim(cells, 0, width, axis=dim)
        tail = lax.slice_in_dim(cells, cells.shape[dim] - width, cells.shape[dim], axis=dim)
        cells = jnp.concatenate(
            [
                lax.ppermute(tail, axis, [(i, (i + 1) % count) for i in range(ends)]),
                cells,
                lax.ppermute(head, axis, [((i + 1) % count, i) for i in range(ends)]),
            ],
            axis=dim,
        )
    return cells


def widen_rim(field):
    return extended(field, (("along", 0), ("across", 1)), 2)


def spread(field, local_coef):
    rows_here, cols_here = (field.shape[0], field.shape[1])
    padded = widen_rim(field)
    result = jnp.zeros(field.shape, jnp.float32)
    for row_shift in range(5):
        for col_shift in range(5):
            result = (
                result
                + local_coef[row_shift * 5 + col_shift]
                * padded[row_shift : row_shift + rows_here, col_shift : col_shift + cols_here]
            )
    return result


def spread_back(field, local_coef):
    rows_here, cols_here = (field.shape[0], field.shape[1])
    padded = widen_rim(field)
    result = jnp.zeros(field.shape, jnp.float32)
    for row_shift in range(5):
        for col_shift in range(5):
            result = (
                result
                + local_coef[row_shift * 5 + col_shift]
                * padded[
                    4 - row_shift : 4 - row_shift + rows_here,
                    4 - col_shift : 4 - col_shift + cols_here,
                ]
            )
    return result


def on_device(jacobian, departures, inv_variance, channel_use, clear_flags, coefficients):
    weight = (
        inv_variance[None, None, :]
        * channel_use.astype(jnp.float32)[None, None, :]
        * clear_flags.astype(jnp.float32)[:, :, None]
    )

    def forward(field):
        return jnp.einsum("xycs,xys->xyc", jacobian, field, precision=lax.Precision.HIGHEST)

    def back_project(weighted):
        adjoint_obs = jnp.einsum(
            "xycs,xyc->xys", jacobian, weighted, precision=lax.Precision.HIGHEST
        )
        return lax.psum(adjoint_obs, "chan")

    def hessian(direction):
        return direction + spread_back(
            back_project(weight * forward(spread(direction, coefficients))), coefficients
        )

    def inner_pair(first, second, third, fourth):
        return lax.psum((jnp.sum(first * second), jnp.sum(third * fourth)), ("along", "across"))

    rhs = spread_back(back_project(weight * departures), coefficients)
    control = jnp.zeros_like(rhs)
    image = hessian(rhs)
    norm_now, product = inner_pair(rhs, rhs, rhs, image)
    alpha = norm_now / product

    def cg_step(step_index, state_tuple):
        control, residual, direction, conj_image, norm_now, alpha = state_tuple
        control = control + alpha * direction
        residual = residual - alpha * conj_image
        image = hessian(residual)
        fresh_norm, product = inner_pair(residual, residual, residual, image)
        beta_ratio = fresh_norm / norm_now
        alpha_next = fresh_norm / (product - beta_ratio * fresh_norm / alpha)
        direction = residual + beta_ratio * direction
        conj_image = image + beta_ratio * conj_image
        return (control, residual, direction, conj_image, fresh_norm, alpha_next)

    control, residual, direction, conj_image, norm_now, alpha = lax.fori_loop(
        0, ITERS - 1, cg_step, (control, rhs, rhs, image, norm_now, alpha)
    )
    control = control + alpha * direction
    residual = residual - alpha * conj_image
    increment = spread(control, coefficients)
    return (control, increment, residual)


def solution(mesh):
    return jax.shard_map(
        on_device,
        mesh=mesh,
        in_specs=(
            P("along", "across", "chan", None),
            P("along", "across", "chan"),
            P("chan"),
            P("chan"),
            P("along", "across"),
            P(),
        ),
        out_specs=(
            P("along", "across", None),
            P("along", "across", None),
            P("along", "across", None),
        ),
        check_vma=False,
    )
```

profile of v0, /device:TPU:0, one launch (start us, length us, event | category | flops | bytes accessed | tf_op | source)
XLA Modules:
  0.0 830.2 jit_solution(16266260684753608233)
XLA Ops:
  2.8 5.8 fusion.298
  8.6 21.3 %psum.49 = f32[4,8,384]{2,1,0:T(8,128)S(1)} all-reduce(f32[4,8,384]{2,1,0:T(8,128)S(1)} %bitcast.53), channel_id=1, replica_groups=mesh['along'=2,'across'=4,'chan'=4] {'chan'}, use_global_device_ids=true, to_apply=%region_0.0 | all-reduce | flops 12288 | bytes 98304 | tf_op jit(solution)/shard_map/psum | solution.py:75
  52.1 5.6 collective-permute-done.15
  57.9 8.7 %fusion.284 = f32[4,8,1,128]{3,2,1,0:T(1,128)S(1)} fusion(f32[4,8,128,384]{3,2,1,0:T(8,128)} %param.8, f32[4,8,384,1]{2,1,0,3:T(8,128)S(1)} %fusion.135), kind=kOutput, calls=%fused_computation.537 | convolution fusion | flops 18874368 | bytes 6356992 | tf_op jit(solution)/shard_map/xycs,xys->xyc/dot_general | solution.py:69
  70.4 16.2 %psum.50 = f32[4,8,384]{2,1,0:T(8,128)S(1)} all-reduce(f32[4,8,384]{2,1,0:T(8,128)S(1)} %bitcast.54), channel_id=1, replica_groups=mesh['along'=2,'across'=4,'chan'=4] {'chan'}, use_global_device_ids=true, to_apply=%region_1.0 | all-reduce | flops 12288 | bytes 98304 | tf_op jit(solution)/shard_map/psum | solution.py:75
  92.3 5.3 collective-permute-start.19
  99.9 17.4 %all-reduce.1 = (f32[]{:T(128)}, f32[]{:T(128)}) all-reduce(f32[]{:T(128)} %get-tuple-element.132, f32[]{:T(128)} %get-tuple-element.131), channel_id=1, replica_groups=mesh['along'=2,'across'=4,'chan'=4] {'along','across'}, use_global_device_ids=true, to_apply=%region_3.0 | all-reduce | flops 2 | bytes 16 | tf_op jit(solution)/shard_map/psum | solution.py:83
  118.6 697.0 %while.21 = (s32[]{:T(128)}, f32[4,8,384]{2,1,0:T(8,128)S(1)}, f32[4,8,384]{2,1,0:T(8,128)S(1)}, f32[4,8,384]{2,1,0:T(8,128)S(1)}, f32[4,8,384]{2,1,0:T(8,128)S(...) while((s32[]{:T(128)}, f32[4,8,384]{2,1,0:T(8,128)S(1)}, ...), condition=%wide.region_12.0_spmd.clone, body=%wide.region_6.0_spmd.clone.sunk | while | flops 39649280 | bytes 42392784 | solution.py:103
  134.2 8.7 %fusion.324 = f32[4,8,1,128]{3,2,1,0:T(1,128)S(1)} fusion(f32[4,8,128,384]{3,2,1,0:T(8,128)} %get-tuple-element.441, f32[4,8,384,1]{2,1,0,3:T(8,128)S(1)} %fusion.323), kind=kOutput, calls=%fused_computation.166.clone.1 | convolution fusion | flops 18874368 | bytes 6356992 | tf_op jit(solution)/shard_map/while/body/eval_jaxpr/xycs,xys->xyc/dot_general | solution.py:69
  146.7 17.9 %psum.57 = f32[4,8,384]{2,1,0:T(8,128)S(1)} all-reduce(f32[4,8,384]{2,1,0:T(8,128)S(1)} %bitcast.50), channel_id=1, replica_groups=mesh['along'=2,'across'=4,'chan'=4] {'chan'}, use_global_device_ids=true, to_apply=%region_9.0 | all-reduce | flops 12288 | bytes 98304 | tf_op jit(solution)/shard_map/while/body/eval_jaxpr/psum | solution.py:75
  179.3 15.4 %all-reduce.3 = (f32[]{:T(128)}, f32[]{:T(128)}) all-reduce(f32[]{:T(128)} %get-tuple-element.399, f32[]{:T(128)} %get-tuple-element.400), channel_id=1, replica_groups=mesh['along'=2,'across'=4,'chan'=4] {'along','across'}, use_global_device_ids=true, to_apply=%region_8.0 | all-reduce | flops 2 | bytes 16 | tf_op jit(solution)/shard_map/while/body/eval_jaxpr/psum | solution.py:83
  206.8 5.4 collective-permute-done.3
  212.4 8.7 %fusion.324 = f32[4,8,1,128]{3,2,1,0:T(1,128)S(1)} fusion(f32[4,8,128,384]{3,2,1,0:T(8,128)} %get-tuple-element.441, f32[4,8,384,1]{2,1,0,3:T(8,128)S(1)} %fusion.323), kind=kOutput, calls=%fused_computation.166.clone.1 | convolution fusion | flops 18874368 | bytes 6356992 | tf_op jit(solution)/shard_map/while/body/eval_jaxpr/xycs,xys->xyc/dot_general | solution.py:69
  224.8 16.5 %psum.57 = f32[4,8,384]{2,1,0:T(8,128)S(1)} all-reduce(f32[4,8,384]{2,1,0:T(8,128)S(1)} %bitcast.50), channel_id=1, replica_groups=mesh['along'=2,'across'=4,'chan'=4] {'chan'}, use_global_device_ids=true, to_apply=%region_9.0 | all-reduce | flops 12288 | bytes 98304 | tf_op jit(solution)/shard_map/while/body/eval_jaxpr/psum | solution.py:75
  256.8 14.3 %all-reduce.3 = (f32[]{:T(128)}, f32[]{:T(128)}) all-reduce(f32[]{:T(128)} %get-tuple-element.399, f32[]{:T(128)} %get-tuple-element.400), channel_id=1, replica_groups=mesh['along'=2,'across'=4,'chan'=4] {'along','across'}, use_global_device_ids=true, to_apply=%region_8.0 | all-reduce | flops 2 | bytes 16 | tf_op jit(solution)/shard_map/while/body/eval_jaxpr/psum | solution.py:83
  283.8 4.9 collective-permute-done.3
  288.9 8.7 %fusion.324 = f32[4,8,1,128]{3,2,1,0:T(1,128)S(1)} fusion(f32[4,8,128,384]{3,2,1,0:T(8,128)} %get-tuple-element.441, f32[4,8,384,1]{2,1,0,3:T(8,128)S(1)} %fusion.323), kind=kOutput, calls=%fused_computation.166.clone.1 | convolution fusion | flops 18874368 | bytes 6356992 | tf_op jit(solution)/shard_map/while/body/eval_jaxpr/xycs,xys->xyc/dot_general | solution.py:69
  301.3 17.8 %psum.57 = f32[4,8,384]{2,1,0:T(8,128)S(1)} all-reduce(f32[4,8,384]{2,1,0:T(8,128)S(1)} %bitcast.50), channel_id=1, replica_groups=mesh['along'=2,'across'=4,'chan'=4] {'chan'}, use_global_device_ids=true, to_apply=%region_9.0 | all-reduce | flops 12288 | bytes 98304 | tf_op jit(solution)/shard_map/while/body/eval_jaxpr/psum | solution.py:75
  323.6 4.8 collective-permute-start.6
  334.9 14.3 %all-reduce.3 = (f32[]{:T(128)}, f32[]{:T(128)}) all-reduce(f32[]{:T(128)} %get-tuple-element.399, f32[]{:T(128)} %get-tuple-element.400), channel_id=1, replica_groups=mesh['along'=2,'across'=4,'chan'=4] {'along','across'}, use_global_device_ids=true, to_apply=%region_8.0 | all-reduce | flops 2 | bytes 16 | tf_op jit(solution)/shard_map/while/body/eval_jaxpr/psum | solution.py:83
  361.9 4.9 collective-permute-done.3
  367.0 8.7 %fusion.324 = f32[4,8,1,128]{3,2,1,0:T(1,128)S(1)} fusion(f32[4,8,128,384]{3,2,1,0:T(8,128)} %get-tuple-element.441, f32[4,8,384,1]{2,1,0,3:T(8,128)S(1)} %fusion.323), kind=kOutput, calls=%fused_computation.166.clone.1 | convolution fusion | flops 18874368 | bytes 6356992 | tf_op jit(solution)/shard_map/while/body/eval_jaxpr/xycs,xys->xyc/dot_general | solution.py:69
  379.4 16.5 %psum.57 = f32[4,8,384]{2,1,0:T(8,128)S(1)} all-reduce(f32[4,8,384]{2,1,0:T(8,128)S(1)} %bitcast.50), channel_id=1, replica_groups=mesh['along'=2,'across'=4,'chan'=4] {'chan'}, use_global_device_ids=true, to_apply=%region_9.0 | all-reduce | flops 12288 | bytes 98304 | tf_op jit(solution)/shard_map/while/body/eval_jaxpr/psum | solution.py:75
  400.3 4.6 collective-permute-start.6
  411.4 14.3 %all-reduce.3 = (f32[]{:T(128)}, f32[]{:T(128)}) all-reduce(f32[]{:T(128)} %get-tuple-element.399, f32[]{:T(128)} %get-tuple-element.400), channel_id=1, replica_groups=mesh['along'=2,'across'=4,'chan'=4] {'along','across'}, use_global_device_ids=true, to_apply=%region_8.0 | all-reduce | flops 2 | bytes 16 | tf_op jit(solution)/shard_map/while/body/eval_jaxpr/psum | solution.py:83
  438.4 4.9 collective-permute-done.3
  443.5 8.7 %fusion.324 = f32[4,8,1,128]{3,2,1,0:T(1,128)S(1)} fusion(f32[4,8,128,384]{3,2,1,0:T(8,128)} %get-tuple-element.441, f32[4,8,384,1]{2,1,0,3:T(8,128)S(1)} %fusion.323), kind=kOutput, calls=%fused_computation.166.clone.1 | convolution fusion | flops 18874368 | bytes 6356992 | tf_op jit(solution)/shard_map/while/body/eval_jaxpr/xycs,xys->xyc/dot_general | solution.py:69
  455.9 17.8 %psum.57 = f32[4,8,384]{2,1,0:T(8,128)S(1)} all-reduce(f32[4,8,384]{2,1,0:T(8,128)S(1)} %bitcast.50), channel_id=1, replica_groups=mesh['along'=2,'across'=4,'chan'=4] {'chan'}, use_global_device_ids=true, to_apply=%region_9.0 | all-reduce | flops 12288 | bytes 98304 | tf_op jit(solution)/shard_map/while/body/eval_jaxpr/psum | solution.py:75
  478.1 4.8 collective-permute-start.6
  489.5 14.3 %all-reduce.3 = (f32[]{:T(128)}, f32[]{:T(128)}) all-reduce(f32[]{:T(128)} %get-tuple-element.399, f32[]{:T(128)} %get-tuple-element.400), channel_id=1, replica_groups=mesh['along'=2,'across'=4,'chan'=4] {'along','across'}, use_global_device_ids=true, to_apply=%region_8.0 | all-reduce | flops 2 | bytes 16 | tf_op jit(solution)/shard_map/while/body/eval_jaxpr/psum | solution.py:83
  516.4 4.9 collective-permute-done.3
  521.5 8.7 %fusion.324 = f32[4,8,1,128]{3,2,1,0:T(1,128)S(1)} fusion(f32[4,8,128,384]{3,2,1,0:T(8,128)} %get-tuple-element.441, f32[4,8,384,1]{2,1,0,3:T(8,128)S(1)} %fusion.323), kind=kOutput, calls=%fused_computation.166.clone.1 | convolution fusion | flops 18874368 | bytes 6356992 | tf_op jit(solution)/shard_map/while/body/eval_jaxpr/xycs,xys->xyc/dot_general | solution.py:69
  534.0 16.5 %psum.57 = f32[4,8,384]{2,1,0:T(8,128)S(1)} all-reduce(f32[4,8,384]{2,1,0:T(8,128)S(1)} %bitcast.50), channel_id=1, replica_groups=mesh['along'=2,'across'=4,'chan'=4] {'chan'}, use_global_device_ids=true, to_apply=%region_9.0 | all-reduce | flops 12288 | bytes 98304 | tf_op jit(solution)/shard_map/while/body/eval_jaxpr/psum | solution.py:75
  566.0 14.3 %all-reduce.3 = (f32[]{:T(128)}, f32[]{:T(128)}) all-reduce(f32[]{:T(128)} %get-tuple-element.399, f32[]{:T(128)} %get-tuple-element.400), channel_id=1, replica_groups=mesh['along'=2,'across'=4,'chan'=4] {'along','across'}, use_global_device_ids=true, to_apply=%region_8.0 | all-reduce | flops 2 | bytes 16 | tf_op jit(solution)/shard_map/while/body/eval_jaxpr/psum | solution.py:83
  592.9 4.9 collective-permute-done.3
  598.0 8.7 %fusion.324 = f32[4,8,1,128]{3,2,1,0:T(1,128)S(1)} fusion(f32[4,8,128,384]{3,2,1,0:T(8,128)} %get-tuple-element.441, f32[4,8,384,1]{2,1,0,3:T(8,128)S(1)} %fusion.323), kind=kOutput, calls=%fused_computation.166.clone.1 | convolution fusion | flops 18874368 | bytes 6356992 | tf_op jit(solution)/shard_map/while/body/eval_jaxpr/xycs,xys->xyc/dot_general | solution.py:69
  610.5 17.8 %psum.57 = f32[4,8,384]{2,1,0:T(8,128)S(1)} all-reduce(f32[4,8,384]{2,1,0:T(8,128)S(1)} %bitcast.50), channel_id=1, replica_groups=mesh['along'=2,'across'=4,'chan'=4] {'chan'}, use_global_device_ids=true, to_apply=%region_9.0 | all-reduce | flops 12288 | bytes 98304 | tf_op jit(solution)/shard_map/while/body/eval_jaxpr/psum | solution.py:75
  632.7 4.8 collective-permute-start.6
  644.0 14.3 %all-reduce.3 = (f32[]{:T(128)}, f32[]{:T(128)}) all-reduce(f32[]{:T(128)} %get-tuple-element.399, f32[]{:T(128)} %get-tuple-element.400), channel_id=1, replica_groups=mesh['along'=2,'across'=4,'chan'=4] {'along','across'}, use_global_device_ids=true, to_apply=%region_8.0 | all-reduce | flops 2 | bytes 16 | tf_op jit(solution)/shard_map/while/body/eval_jaxpr/psum | solution.py:83
  671.0 4.9 collective-permute-done.3
  676.1 8.7 %fusion.324 = f32[4,8,1,128]{3,2,1,0:T(1,128)S(1)} fusion(f32[4,8,128,384]{3,2,1,0:T(8,128)} %get-tuple-element.441, f32[4,8,384,1]{2,1,0,3:T(8,128)S(1)} %fusion.323), kind=kOutput, calls=%fused_computation.166.clone.1 | convolution fusion | flops 18874368 | bytes 6356992 | tf_op jit(solution)/shard_map/while/body/eval_jaxpr/xycs,xys->xyc/dot_general | solution.py:69
  688.5 16.5 %psum.57 = f32[4,8,384]{2,1,0:T(8,128)S(1)} all-reduce(f32[4,8,384]{2,1,0:T(8,128)S(1)} %bitcast.50), channel_id=1, replica_groups=mesh['along'=2,'across'=4,'chan'=4] {'chan'}, use_global_device_ids=true, to_apply=%region_9.0 | all-reduce | flops 12288 | bytes 98304 | tf_op jit(solution)/shard_map/while/body/eval_jaxpr/psum | solution.py:75
  720.5 14.3 %all-reduce.3 = (f32[]{:T(128)}, f32[]{:T(128)}) all-reduce(f32[]{:T(128)} %get-tuple-element.399, f32[]{:T(128)} %get-tuple-element.400), channel_id=1, replica_groups=mesh['along'=2,'across'=4,'chan'=4] {'along','across'}, use_global_device_ids=true, to_apply=%region_8.0 | all-reduce | flops 2 | bytes 16 | tf_op jit(solution)/shard_map/while/body/eval_jaxpr/psum | solution.py:83
  747.5 4.9 collective-permute-done.3
  752.6 8.7 %fusion.324 = f32[4,8,1,128]{3,2,1,0:T(1,128)S(1)} fusion(f32[4,8,128,384]{3,2,1,0:T(8,128)} %get-tuple-element.441, f32[4,8,384,1]{2,1,0,3:T(8,128)S(1)} %fusion.323), kind=kOutput, calls=%fused_computation.166.clone.1 | convolution fusion | flops 18874368 | bytes 6356992 | tf_op jit(solution)/shard_map/while/body/eval_jaxpr/xycs,xys->xyc/dot_general | solution.py:69
  765.1 17.8 %psum.57 = f32[4,8,384]{2,1,0:T(8,128)S(1)} all-reduce(f32[4,8,384]{2,1,0:T(8,128)S(1)} %bitcast.50), channel_id=1, replica_groups=mesh['along'=2,'across'=4,'chan'=4] {'chan'}, use_global_device_ids=true, to_apply=%region_9.0 | all-reduce | flops 12288 | bytes 98304 | tf_op jit(solution)/shard_map/while/body/eval_jaxpr/psum | solution.py:75
  787.3 4.8 collective-permute-start.6
  798.6 14.3 %all-reduce.3 = (f32[]{:T(128)}, f32[]{:T(128)}) all-reduce(f32[]{:T(128)} %get-tuple-element.399, f32[]{:T(128)} %get-tuple-element.400), channel_id=1, replica_groups=mesh['along'=2,'across'=4,'chan'=4] {'along','across'}, use_global_device_ids=true, to_apply=%region_8.0 | all-reduce | flops 2 | bytes 16 | tf_op jit(solution)/shard_map/while/body/eval_jaxpr/psum | solution.py:83
  (374 shorter events, 289.4 us)
Async XLA Ops:
  34.3 5.9 collective-permute-start.10
  35.6 6.1 collective-permute-start.11
  46.3 5.9 collective-permute-start.14
  50.6 7.2 collective-permute-start.15
  91.0 6.7 collective-permute-start.18
  92.3 6.8 collective-permute-start.19
  118.7 4.7 collective-permute-start
  124.1 5.7 collective-permute-start.2
  128.3 5.7 collective-permute-start.3
  169.0 5.7 collective-permute-start.6
  172.8 5.7 collective-permute-start.7
  197.4 4.8 collective-permute-start
  205.3 6.9 collective-permute-start.3
  245.7 6.5 collective-permute-start.6
  250.3 5.7 collective-permute-start.7
  273.9 4.8 collective-permute-start
  279.5 4.3 collective-permute-start.2
  282.3 6.4 collective-permute-start.3
  323.6 6.8 collective-permute-start.6
  328.4 5.7 collective-permute-start.7
  352.0 4.8 collective-permute-start
  357.5 4.3 collective-permute-start.2
  360.3 6.4 collective-permute-start.3
  400.3 6.5 collective-permute-start.6
  404.9 5.7 collective-permute-start.7
  428.5 4.8 collective-permute-start
  434.1 4.3 collective-permute-start.2
  436.9 6.4 collective-permute-start.3
  478.1 6.8 collective-permute-start.6
  482.9 5.7 collective-permute-start.7
  506.5 4.8 collective-permute-start
  512.1 4.3 collective-permute-start.2
  514.9 6.4 collective-permute-start.3
  554.9 6.5 collective-permute-start.6
  559.5 5.7 collective-permute-start.7
  583.0 4.8 collective-permute-start
  591.4 6.4 collective-permute-start.3
  632.7 6.8 collective-permute-start.6
  637.5 5.7 collective-permute-start.7
  661.1 4.8 collective-permute-start
  669.5 6.4 collective-permute-start.3
  709.4 6.5 collective-permute-start.6
  714.0 5.7 collective-permute-start.7
  737.6 4.8 collective-permute-start
  746.0 6.4 collective-permute-start.3
  787.3 6.8 collective-permute-start.6
  792.1 5.7 collective-permute-start.7
  823.0 6.4 collective-permute-start.23
  (53 other events, 473.4 us)
where the time goes:
time: 833 us; the launch traced here: 830 us
  blocking collectives  340 us (41%)
  starting transfers between devices  189 us (23%)
  matrix products  129 us (15%)
  waiting for transfers between devices  122 us (15%)
  loops' own time  31.3 us (4%)
  other arithmetic  14.8 us (2%)
    psum x11, blocking collectives, back_project(): return lax.psum(adjoint_obs, 'chan')  192 us
    psum x10, blocking collectives, inner_pair(): lax.psum((jnp.sum(first * second), jnp.sum(third * fourth)), ('along', 'a...  147 us
    ppermute x44, starting transfers between devices, extended(): lax.ppermute(tail, axis, [(i, (i + 1) % count) for i in range(ends)])  130 us
    ppermute x44, waiting for transfers between devices, extended(): lax.ppermute(head, axis, [((i + 1) % count, i) for i in range(ends)])  111 us
    dot_general x10, matrix products, forward(): jnp.einsum('xycs,xys->xyc', jacobian, field, precision=lax.Precision.HIGH...  87.2 us
    ppermute x44, starting transfers between devices, extended(): lax.ppermute(head, axis, [((i + 1) % count, i) for i in range(ends)])  59.5 us
    dot_general x11, matrix products, back_project(): jnp.einsum('xycs,xyc->xys', jacobian, weighted, precision=lax.Precision.H...  42.1 us
    another operation x1, loops' own time, on_device(): lax.fori_loop(0, ITERS - 1, cg_step, (control, rhs, rhs, image, norm_now,...  31.3 us
  transfers between devices with their start and end apart: 88, of which 53 were waited for; matrix products, arithmetic and copies ran while one was open for 0% of the time, Pallas kernels for 0%

commit v1 on v0

--- a/solution.py
+++ b/solution.py
@@ -72,7 +72,7 @@
         adjoint_obs = jnp.einsum(
             "xycs,xyc->xys", jacobian, weighted, precision=lax.Precision.HIGHEST
         )
-        return lax.psum(adjoint_obs, "chan")
+        return jnp.sum(lax.all_gather(adjoint_obs, "chan"), axis=0)
 
     def hessian(direction):
         return direction + spread_back(

time: 833 us -> 801 us (0.962)
  waiting for transfers between devices: 122 us -> 80.2 us
  starting transfers between devices: 189 us -> 216 us
  blocking collectives: 340 us -> 322 us
    psum x11 -> x0, blocking collectives: 192 us -> none  [back_project(): return lax.psum(adjoint_obs, 'chan')]
    all_gather x0 -> x11, blocking collectives: none -> 152 us  [back_project(): return jnp.sum(lax.all_gather(adjoint_obs, 'chan'), axis=0)]
    ppermute x44, waiting for transfers between devices: 111 us -> 54.2 us  [extended(): lax.ppermute(head, axis, [((i + 1) % count, i) for i in range(ends)])]
    ppermute x44, starting transfers between devices: 130 us -> 157 us  [extended(): lax.ppermute(tail, axis, [(i, (i + 1) % count) for i in range(ends)])]
    psum x10, blocking collectives: 147 us -> 170 us  [inner_pair(): lax.psum((jnp.sum(first * second), jnp.sum(third * fourth)), ('along', 'a...]
    ppermute x44, waiting for transfers between devices: 10.9 us -> 26 us  [extended(): lax.ppermute(tail, axis, [(i, (i + 1) % count) for i in range(ends)])]
  transfers between devices with their start and end apart: 88 -> 88, of which waited for: 53 -> 54; matrix products, arithmetic and copies ran while one was open for 0% -> 0% of each run, Pallas kernels for 0% -> 0%
where the time goes in v1:
time: 801 us; the launch traced here: 798 us
  blocking collectives  322 us (40%)
  starting transfers between devices  216 us (27%)
  matrix products  129 us (16%)
  waiting for transfers between devices  80.2 us (10%)
  loops' own time  31.1 us (4%)
  other arithmetic  15.2 us (2%)
    psum x10, blocking collectives, inner_pair(): lax.psum((jnp.sum(first * second), jnp.sum(third * fourth)), ('along', 'a...  170 us
    ppermute x44, starting transfers between devices, extended(): lax.ppermute(tail, axis, [(i, (i + 1) % count) for i in range(ends)])  157 us
    all_gather x11, blocking collectives, back_project(): return jnp.sum(lax.all_gather(adjoint_obs, 'chan'), axis=0)  152 us
    dot_general x10, matrix products, forward(): jnp.einsum('xycs,xys->xyc', jacobian, field, precision=lax.Precision.HIGH...  87.2 us
    ppermute x44, starting transfers between devices, extended(): lax.ppermute(head, axis, [((i + 1) % count, i) for i in range(ends)])  59.2 us
    ppermute x44, waiting for transfers between devices, extended(): lax.ppermute(head, axis, [((i + 1) % count, i) for i in range(ends)])  54.2 us
    dot_general x11, matrix products, back_project(): jnp.einsum('xycs,xyc->xys', jacobian, weighted, precision=lax.Precision.H...  42.1 us
    another operation x1, loops' own time, on_device(): lax.fori_loop(0, ITERS - 1, cg_step, (control, rhs, rhs, image, norm_now,...  31.1 us
  transfers between devices with their start and end apart: 88, of which 54 were waited for; matrix products, arithmetic and copies ran while one was open for 0% of the time, Pallas kernels for 0%

profile of v1, /device:TPU:0, one launch (start us, length us, event | category | flops | bytes accessed | tf_op | source)
XLA Modules:
  0.0 798.2 jit_solution(8011080568190956837)
XLA Ops:
  2.8 5.8 fusion.199
  8.6 15.5 %all-gather.1 = f32[16,8,384]{2,1,0:T(8,128)S(1)} all-gather(f32[4,8,384]{2,1,0:T(8,128)S(1)} %bitcast.61), channel_id=3, replica_groups=mesh['along'=2,'across'=4,'chan'=4] {'chan'}, dimensions={0}, use_global_device_ids=true | all-gather | bytes 245760 | tf_op jit(solution)/shard_map/all_gather | solution.py:75
  29.8 4.5 collective-permute-start.11
  40.8 4.3 collective-permute-start.14
  46.6 5.4 collective-permute-done.15
  52.2 8.7 %fusion.188 = f32[4,8,1,128]{3,2,1,0:T(1,128)S(1)} fusion(f32[4,8,128,384]{3,2,1,0:T(8,128)} %param.8, f32[4,8,384,1]{2,1,0,3:T(8,128)S(1)} %fusion.131), kind=kOutput, calls=%fused_computation.395 | convolution fusion | flops 18874368 | bytes 6356992 | tf_op jit(solution)/shard_map/xycs,xys->xyc/dot_general | solution.py:69
  64.6 13.7 %all-gather.2 = f32[16,8,384]{2,1,0:T(8,128)S(1)} all-gather(f32[4,8,384]{2,1,0:T(8,128)S(1)} %bitcast.62), channel_id=4, replica_groups=mesh['along'=2,'across'=4,'chan'=4] {'chan'}, dimensions={0}, use_global_device_ids=true | all-gather | bytes 245760 | tf_op jit(solution)/shard_map/all_gather | solution.py:75
  84.0 5.5 collective-permute-start.19
  91.8 17.4 %all-reduce.1 = (f32[]{:T(128)}, f32[]{:T(128)}) all-reduce(f32[]{:T(128)} %get-tuple-element.132, f32[]{:T(128)} %get-tuple-element.131), channel_id=1, replica_groups=mesh['along'=2,'across'=4,'chan'=4] {'along','across'}, use_global_device_ids=true, to_apply=%region_3.0 | all-reduce | flops 2 | bytes 16 | tf_op jit(solution)/shard_map/psum | solution.py:83
  110.5 672.5 %while.21 = (s32[]{:T(128)}, f32[4,8,384]{2,1,0:T(8,128)S(1)}, f32[4,8,384]{2,1,0:T(8,128)S(1)}, f32[4,8,384]{2,1,0:T(8,128)S(1)}, f32[4,8,384]{2,1,0:T(8,128)S(...) while((s32[]{:T(128)}, f32[4,8,384]{2,1,0:T(8,128)S(1)}, ...), condition=%wide.region_12.0_spmd.clone, body=%wide.region_6.0_spmd.clone.sunk | while | flops 39686144 | bytes 43572444 | solution.py:103
  121.7 4.2 collective-permute-done.3
  126.1 8.7 %fusion.224 = f32[4,8,1,128]{3,2,1,0:T(1,128)S(1)} fusion(f32[4,8,128,384]{3,2,1,0:T(8,128)} %get-tuple-element.418, f32[4,8,384,1]{2,1,0,3:T(8,128)S(1)} %fusion.223), kind=kOutput, calls=%fused_computation.120.clone.1 | convolution fusion | flops 18874368 | bytes 6356992 | tf_op jit(solution)/shard_map/while/body/eval_jaxpr/xycs,xys->xyc/dot_general | solution.py:69
  138.6 13.7 %all-gather.5 = f32[16,8,384]{2,1,0:T(8,128)S(1)} all-gather(f32[4,8,384]{2,1,0:T(8,128)S(1)} %bitcast.56), channel_id=2, replica_groups=mesh['along'=2,'across'=4,'chan'=4] {'chan'}, dimensions={0}, use_global_device_ids=true | all-gather | bytes 245760 | tf_op jit(solution)/shard_map/while/body/eval_jaxpr/all_gather | solution.py:75
  158.8 4.5 collective-permute-start.7
  165.6 17.0 %all-reduce.3 = (f32[]{:T(128)}, f32[]{:T(128)}) all-reduce(f32[]{:T(128)} %get-tuple-element.374, f32[]{:T(128)} %get-tuple-element.375), channel_id=1, replica_groups=mesh['along'=2,'across'=4,'chan'=4] {'along','across'}, use_global_device_ids=true, to_apply=%region_8.0 | all-reduce | flops 2 | bytes 16 | tf_op jit(solution)/shard_map/while/body/eval_jaxpr/psum | solution.py:83
  196.5 4.2 collective-permute-done.3
  200.9 8.7 %fusion.224 = f32[4,8,1,128]{3,2,1,0:T(1,128)S(1)} fusion(f32[4,8,128,384]{3,2,1,0:T(8,128)} %get-tuple-element.418, f32[4,8,384,1]{2,1,0,3:T(8,128)S(1)} %fusion.223), kind=kOutput, calls=%fused_computation.120.clone.1 | convolution fusion | flops 18874368 | bytes 6356992 | tf_op jit(solution)/shard_map/while/body/eval_jaxpr/xycs,xys->xyc/dot_general | solution.py:69
  213.3 13.6 %all-gather.5 = f32[16,8,384]{2,1,0:T(8,128)S(1)} all-gather(f32[4,8,384]{2,1,0:T(8,128)S(1)} %bitcast.56), channel_id=2, replica_groups=mesh['along'=2,'across'=4,'chan'=4] {'chan'}, dimensions={0}, use_global_device_ids=true | all-gather | bytes 245760 | tf_op jit(solution)/shard_map/while/body/eval_jaxpr/all_gather | solution.py:75
  233.5 4.5 collective-permute-start.7
  240.3 17.0 %all-reduce.3 = (f32[]{:T(128)}, f32[]{:T(128)}) all-reduce(f32[]{:T(128)} %get-tuple-element.374, f32[]{:T(128)} %get-tuple-element.375), channel_id=1, replica_groups=mesh['along'=2,'across'=4,'chan'=4] {'along','across'}, use_global_device_ids=true, to_apply=%region_8.0 | all-reduce | flops 2 | bytes 16 | tf_op jit(solution)/shard_map/while/body/eval_jaxpr/psum | solution.py:83
  275.6 8.7 %fusion.224 = f32[4,8,1,128]{3,2,1,0:T(1,128)S(1)} fusion(f32[4,8,128,384]{3,2,1,0:T(8,128)} %get-tuple-element.418, f32[4,8,384,1]{2,1,0,3:T(8,128)S(1)} %fusion.223), kind=kOutput, calls=%fused_computation.120.clone.1 | convolution fusion | flops 18874368 | bytes 6356992 | tf_op jit(solution)/shard_map/while/body/eval_jaxpr/xycs,xys->xyc/dot_general | solution.py:69
  288.0 13.6 %all-gather.5 = f32[16,8,384]{2,1,0:T(8,128)S(1)} all-gather(f32[4,8,384]{2,1,0:T(8,128)S(1)} %bitcast.56), channel_id=2, replica_groups=mesh['along'=2,'across'=4,'chan'=4] {'chan'}, dimensions={0}, use_global_device_ids=true | all-gather | bytes 245760 | tf_op jit(solution)/shard_map/while/body/eval_jaxpr/all_gather | solution.py:75
  308.2 4.5 collective-permute-start.7
  315.1 17.0 %all-reduce.3 = (f32[]{:T(128)}, f32[]{:T(128)}) all-reduce(f32[]{:T(128)} %get-tuple-element.374, f32[]{:T(128)} %get-tuple-element.375), channel_id=1, replica_groups=mesh['along'=2,'across'=4,'chan'=4] {'along','across'}, use_global_device_ids=true, to_apply=%region_8.0 | all-reduce | flops 2 | bytes 16 | tf_op jit(solution)/shard_map/while/body/eval_jaxpr/psum | solution.py:83
  350.3 8.7 %fusion.224 = f32[4,8,1,128]{3,2,1,0:T(1,128)S(1)} fusion(f32[4,8,128,384]{3,2,1,0:T(8,128)} %get-tuple-element.418, f32[4,8,384,1]{2,1,0,3:T(8,128)S(1)} %fusion.223), kind=kOutput, calls=%fused_computation.120.clone.1 | convolution fusion | flops 18874368 | bytes 6356992 | tf_op jit(solution)/shard_map/while/body/eval_jaxpr/xycs,xys->xyc/dot_general | solution.py:69
  362.8 13.6 %all-gather.5 = f32[16,8,384]{2,1,0:T(8,128)S(1)} all-gather(f32[4,8,384]{2,1,0:T(8,128)S(1)} %bitcast.56), channel_id=2, replica_groups=mesh['along'=2,'across'=4,'chan'=4] {'chan'}, dimensions={0}, use_global_device_ids=true | all-gather | bytes 245760 | tf_op jit(solution)/shard_map/while/body/eval_jaxpr/all_gather | solution.py:75
  382.9 4.5 collective-permute-start.7
  389.8 17.0 %all-reduce.3 = (f32[]{:T(128)}, f32[]{:T(128)}) all-reduce(f32[]{:T(128)} %get-tuple-element.374, f32[]{:T(128)} %get-tuple-element.375), channel_id=1, replica_groups=mesh['along'=2,'across'=4,'chan'=4] {'along','across'}, use_global_device_ids=true, to_apply=%region_8.0 | all-reduce | flops 2 | bytes 16 | tf_op jit(solution)/shard_map/while/body/eval_jaxpr/psum | solution.py:83
  425.0 8.7 %fusion.224 = f32[4,8,1,128]{3,2,1,0:T(1,128)S(1)} fusion(f32[4,8,128,384]{3,2,1,0:T(8,128)} %get-tuple-element.418, f32[4,8,384,1]{2,1,0,3:T(8,128)S(1)} %fusion.223), kind=kOutput, calls=%fused_computation.120.clone.1 | convolution fusion | flops 18874368 | bytes 6356992 | tf_op jit(solution)/shard_map/while/body/eval_jaxpr/xycs,xys->xyc/dot_general | solution.py:69
  437.5 13.6 %all-gather.5 = f32[16,8,384]{2,1,0:T(8,128)S(1)} all-gather(f32[4,8,384]{2,1,0:T(8,128)S(1)} %bitcast.56), channel_id=2, replica_groups=mesh['along'=2,'across'=4,'chan'=4] {'chan'}, dimensions={0}, use_global_device_ids=true | all-gather | bytes 245760 | tf_op jit(solution)/shard_map/while/body/eval_jaxpr/all_gather | solution.py:75
  457.6 4.5 collective-permute-start.7
  464.5 17.0 %all-reduce.3 = (f32[]{:T(128)}, f32[]{:T(128)}) all-reduce(f32[]{:T(128)} %get-tuple-element.374, f32[]{:T(128)} %get-tuple-element.375), channel_id=1, replica_groups=mesh['along'=2,'across'=4,'chan'=4] {'along','across'}, use_global_device_ids=true, to_apply=%region_8.0 | all-reduce | flops 2 | bytes 16 | tf_op jit(solution)/shard_map/while/body/eval_jaxpr/psum | solution.py:83
  499.7 8.7 %fusion.224 = f32[4,8,1,128]{3,2,1,0:T(1,128)S(1)} fusion(f32[4,8,128,384]{3,2,1,0:T(8,128)} %get-tuple-element.418, f32[4,8,384,1]{2,1,0,3:T(8,128)S(1)} %fusion.223), kind=kOutput, calls=%fused_computation.120.clone.1 | convolution fusion | flops 18874368 | bytes 6356992 | tf_op jit(solution)/shard_map/while/body/eval_jaxpr/xycs,xys->xyc/dot_general | solution.py:69
  512.2 13.6 %all-gather.5 = f32[16,8,384]{2,1,0:T(8,128)S(1)} all-gather(f32[4,8,384]{2,1,0:T(8,128)S(1)} %bitcast.56), channel_id=2, replica_groups=mesh['along'=2,'across'=4,'chan'=4] {'chan'}, dimensions={0}, use_global_device_ids=true | all-gather | bytes 245760 | tf_op jit(solution)/shard_map/while/body/eval_jaxpr/all_gather | solution.py:75
  532.3 4.5 collective-permute-start.7
  539.2 17.0 %all-reduce.3 = (f32[]{:T(128)}, f32[]{:T(128)}) all-reduce(f32[]{:T(128)} %get-tuple-element.374, f32[]{:T(128)} %get-tuple-element.375), channel_id=1, replica_groups=mesh['along'=2,'across'=4,'chan'=4] {'along','across'}, use_global_device_ids=true, to_apply=%region_8.0 | all-reduce | flops 2 | bytes 16 | tf_op jit(solution)/shard_map/while/body/eval_jaxpr/psum | solution.py:83
  574.5 8.7 %fusion.224 = f32[4,8,1,128]{3,2,1,0:T(1,128)S(1)} fusion(f32[4,8,128,384]{3,2,1,0:T(8,128)} %get-tuple-element.418, f32[4,8,384,1]{2,1,0,3:T(8,128)S(1)} %fusion.223), kind=kOutput, calls=%fused_computation.120.clone.1 | convolution fusion | flops 18874368 | bytes 6356992 | tf_op jit(solution)/shard_map/while/body/eval_jaxpr/xycs,xys->xyc/dot_general | solution.py:69
  586.9 13.6 %all-gather.5 = f32[16,8,384]{2,1,0:T(8,128)S(1)} all-gather(f32[4,8,384]{2,1,0:T(8,128)S(1)} %bitcast.56), channel_id=2, replica_groups=mesh['along'=2,'across'=4,'chan'=4] {'chan'}, dimensions={0}, use_global_device_ids=true | all-gather | bytes 245760 | tf_op jit(solution)/shard_map/while/body/eval_jaxpr/all_gather | solution.py:75
  607.0 4.5 collective-permute-start.7
  613.9 17.0 %all-reduce.3 = (f32[]{:T(128)}, f32[]{:T(128)}) all-reduce(f32[]{:T(128)} %get-tuple-element.374, f32[]{:T(128)} %get-tuple-element.375), channel_id=1, replica_groups=mesh['along'=2,'across'=4,'chan'=4] {'along','across'}, use_global_device_ids=true, to_apply=%region_8.0 | all-reduce | flops 2 | bytes 16 | tf_op jit(solution)/shard_map/while/body/eval_jaxpr/psum | solution.py:83
  649.2 8.7 %fusion.224 = f32[4,8,1,128]{3,2,1,0:T(1,128)S(1)} fusion(f32[4,8,128,384]{3,2,1,0:T(8,128)} %get-tuple-element.418, f32[4,8,384,1]{2,1,0,3:T(8,128)S(1)} %fusion.223), kind=kOutput, calls=%fused_computation.120.clone.1 | convolution fusion | flops 18874368 | bytes 6356992 | tf_op jit(solution)/shard_map/while/body/eval_jaxpr/xycs,xys->xyc/dot_general | solution.py:69
  661.6 13.6 %all-gather.5 = f32[16,8,384]{2,1,0:T(8,128)S(1)} all-gather(f32[4,8,384]{2,1,0:T(8,128)S(1)} %bitcast.56), channel_id=2, replica_groups=mesh['along'=2,'across'=4,'chan'=4] {'chan'}, dimensions={0}, use_global_device_ids=true | all-gather | bytes 245760 | tf_op jit(solution)/shard_map/while/body/eval_jaxpr/all_gather | solution.py:75
  681.8 4.5 collective-permute-start.7
  688.6 17.0 %all-reduce.3 = (f32[]{:T(128)}, f32[]{:T(128)}) all-reduce(f32[]{:T(128)} %get-tuple-element.374, f32[]{:T(128)} %get-tuple-element.375), channel_id=1, replica_groups=mesh['along'=2,'across'=4,'chan'=4] {'along','across'}, use_global_device_ids=true, to_apply=%region_8.0 | all-reduce | flops 2 | bytes 16 | tf_op jit(solution)/shard_map/while/body/eval_jaxpr/psum | solution.py:83
  723.9 8.7 %fusion.224 = f32[4,8,1,128]{3,2,1,0:T(1,128)S(1)} fusion(f32[4,8,128,384]{3,2,1,0:T(8,128)} %get-tuple-element.418, f32[4,8,384,1]{2,1,0,3:T(8,128)S(1)} %fusion.223), kind=kOutput, calls=%fused_computation.120.clone.1 | convolution fusion | flops 18874368 | bytes 6356992 | tf_op jit(solution)/shard_map/while/body/eval_jaxpr/xycs,xys->xyc/dot_general | solution.py:69
  736.3 13.6 %all-gather.5 = f32[16,8,384]{2,1,0:T(8,128)S(1)} all-gather(f32[4,8,384]{2,1,0:T(8,128)S(1)} %bitcast.56), channel_id=2, replica_groups=mesh['along'=2,'across'=4,'chan'=4] {'chan'}, dimensions={0}, use_global_device_ids=true | all-gather | bytes 245760 | tf_op jit(solution)/shard_map/while/body/eval_jaxpr/all_gather | solution.py:75
  756.5 4.5 collective-permute-start.7
  763.3 17.0 %all-reduce.3 = (f32[]{:T(128)}, f32[]{:T(128)}) all-reduce(f32[]{:T(128)} %get-tuple-element.374, f32[]{:T(128)} %get-tuple-element.375), channel_id=1, replica_groups=mesh['along'=2,'across'=4,'chan'=4] {'along','across'}, use_global_device_ids=true, to_apply=%region_8.0 | all-reduce | flops 2 | bytes 16 | tf_op jit(solution)/shard_map/while/body/eval_jaxpr/psum | solution.py:83
  (363 shorter events, 280.6 us)
Async XLA Ops:
  28.5 5.9 collective-permute-start.10
  29.8 6.1 collective-permute-start.11
  40.8 5.8 collective-permute-start.14
  45.1 6.9 collective-permute-start.15
  82.7 6.8 collective-permute-start.18
  84.0 7.0 collective-permute-start.19
  110.6 4.7 collective-permute-start
  116.0 5.7 collective-permute-start.2
  120.2 5.7 collective-permute-start.3
  157.5 6.5 collective-permute-start.6
  158.8 6.1 collective-permute-start.7
  185.3 4.7 collective-permute-start
  190.8 5.7 collective-permute-start.2
  195.0 5.7 collective-permute-start.3
  232.2 6.5 collective-permute-start.6
  233.5 6.1 collective-permute-start.7
  260.1 4.7 collective-permute-start
  265.5 5.7 collective-permute-start.2
  269.7 5.7 collective-permute-start.3
  306.9 6.5 collective-permute-start.6
  308.2 6.1 collective-permute-start.7
  334.8 4.7 collective-permute-start
  340.2 5.7 collective-permute-start.2
  344.4 5.7 collective-permute-start.3
  381.6 6.5 collective-permute-start.6
  382.9 6.1 collective-permute-start.7
  414.9 5.7 collective-permute-start.2
  419.1 5.7 collective-permute-start.3
  456.3 6.5 collective-permute-start.6
  457.6 6.1 collective-permute-start.7
  489.6 5.7 collective-permute-start.2
  493.8 5.7 collective-permute-start.3
  531.0 6.5 collective-permute-start.6
  532.3 6.1 collective-permute-start.7
  564.4 5.7 collective-permute-start.2
  568.6 5.7 collective-permute-start.3
  605.7 6.5 collective-permute-start.6
  607.0 6.1 collective-permute-start.7
  639.1 5.7 collective-permute-start.2
  643.3 5.7 collective-permute-start.3
  680.5 6.5 collective-permute-start.6
  681.8 6.1 collective-permute-start.7
  713.8 5.7 collective-permute-start.2
  718.0 5.7 collective-permute-start.3
  755.2 6.5 collective-permute-start.6
  756.5 6.1 collective-permute-start.7
  788.1 5.5 collective-permute-start.22
  791.6 5.7 collective-permute-start.23
  (53 other events, 500.0 us)
